TPU v7x, 32 devices: a whole 2x2x4 slice. The times are simulated.
32 devices in a mesh: groups: 2 (over x), seq: 16 (over z, y, core).
Axes of the slice: x: 2, y: 2, z: 4, core: 2. Of those that a mesh axis runs over, the one named last changes fastest.
Arguments:
- enc_input: bfloat16 [8192, 1408], P(('groups', 'seq')), parts along dimension 0, may hold values from -6 to 6
- enc_weight: bfloat16 [2816, 1536], P('seq'), may hold values from -0.109375 to 0.109375
- norm_gain: float32 [1536], replicated, may hold values from 0.5 to 1.5
- q_weight: bfloat16 [1536, 1024], replicated, may hold values from -1 to 1
- kv_weight: bfloat16 [1536, 320], replicated, may hold values from -1 to 1
- out_weight: bfloat16 [1536, 1536], replicated, may hold values from -0.15625 to 0.15625
- dec_weight: float32 [3, 1536], replicated, may hold values from -3 to 3
- track_weight: bfloat16 [192, 1536], P('seq'), may hold values from -0.15625 to 0.15625
- track_grad: bfloat16 [4096, 192], P('groups', 'seq'), parts along dimension 0, may hold values from -6 to 6
- track_index: int32 [384], P('groups'), parts along dimension 0, may hold values from 0 to 191, each once
- track_mask: int32 [384], P('groups'), parts along dimension 0, may hold values 0 or 1
Outputs:
- trunk_out: bfloat16 [4096, 1536], P(('groups', 'seq')), parts along dimension 0
- skip_grad: bfloat16 [4096, 1536], P(('groups', 'seq')), parts along dimension 0
- dec_weight_grad: float32 [6, 1536], P('groups'), parts along dimension 0
There are 2 independent parts, one for each index of `groups`. A program takes and returns all parts, laid end to end along the dimension named above; an argument that names none is the same for every part. Nothing has to cross between parts.
Inputs may be any that keep to these rules, and one draw needn't show every extreme that they name: `track_index`: names every track once.
All inputs are finite; a program needn't handle non-finite values.
Results may differ from a plain program's by a relative error of at most 0.02.
Values may be sent and summed in bfloat16 or wider, within the bound.
No kernel may reach another device: no remote copies, remote signals or barrier semaphores. Data moves between devices by JAX's collectives and lax.ppermute only.
A program may use at most 128 MiB of HBM per device.

v0:
```python
import math
import jax
import jax.numpy as jnp
from jax import lax
from jax.sharding import PartitionSpec as P

HEADS = 8
QK = 128
VDIM = 192
DILATION_SPAN = 8


def with_halo(cells, sides, width):
    for axis, dim in sides:
        count = lax.axis_size(axis)
        ends = count - 1
        head = lax.slice_in_dim(cells, 0, width, axis=dim)
        tail = lax.slice_in_dim(cells, cells.shape[dim] - width, cells.shape[dim], axis=dim)
        cells = jnp.concatenate(
            [
                lax.ppermute(tail, axis, [(i, (i + 1) % count) for i in range(ends)]),
                cells,
                lax.ppermute(head, axis, [((i + 1) % count, i) for i in range(ends)]),
            ],
            axis=dim,
        )
    return cells


def gelu_tanh(values):
    return jax.nn.gelu(values, approximate=True)


def attention(tokens, tok_f, norm_gain, q_weight, kv_weight, out_weight):
    token_rows = tokens.shape[0]
    normed = (
        tok_f * lax.rsqrt(jnp.mean(tok_f * tok_f, axis=-1, keepdims=True) + 1e-06) * norm_gain
    ).astype(jnp.bfloat16)
    query = jnp.dot(normed, q_weight, preferred_element_type=jnp.float32).astype(jnp.bfloat16)
    keyval = jnp.dot(normed, kv_weight, preferred_element_type=jnp.float32).astype(jnp.bfloat16)
    query_rows = query.reshape(token_rows * HEADS, QK)

    def block_update(carry, key_block):
        running_max, running_sum, weighted = carry
        scores = lax.dot_general(
            query_rows,
            key_block[:, :QK],
            (((1,), (1,)), ((), ())),
            preferred_element_type=jnp.float32,
        ) * QK ** (-0.5)
        new_max = jnp.maximum(running_max, jnp.max(scores, axis=1))
        shrink = jnp.exp(running_max - new_max)
        expw = jnp.exp(scores - new_max[:, None])
        running_sum = running_sum * shrink + jnp.sum(expw, axis=1)
        weighted = weighted * shrink[:, None] + jnp.dot(
            expw.astype(jnp.bfloat16), key_block[:, QK:], preferred_element_type=jnp.float32
        )
        return (new_max, running_sum, weighted)

    start_state = (
        jnp.full((token_rows * HEADS,), -1e30, jnp.float32),
        jnp.zeros((token_rows * HEADS,), jnp.float32),
        jnp.zeros((token_rows * HEADS, VDIM), jnp.float32),
    )
    carry = start_state
    piece = lax.all_gather(keyval, "seq", axis=0, tiled=True)
    count = piece.shape[0]

    def step_fn(inner, key_block):
        return (block_update(inner, key_block), 0)

    carry, unused = lax.scan(step_fn, carry, piece.reshape(count // 128, 128, piece.shape[1]))
    running_max, running_sum, weighted = carry
    context = (
        (weighted / running_sum[:, None]).reshape(token_rows, HEADS * VDIM).astype(jnp.bfloat16)
    )
    return (tok_f + jnp.dot(context, out_weight, preferred_element_type=jnp.float32)).astype(
        jnp.bfloat16
    )


def decoder_back(tok_f, dec_weight, track_weight, track_grad, track_index, track_mask):
    token_rows = tok_f.shape[0]
    exchanged = lax.all_to_all(track_grad, "seq", split_axis=0, concat_axis=1, tiled=True)
    masked = exchanged * track_mask.astype(jnp.bfloat16)[None, :]
    every_row = lax.all_gather(track_weight, "seq", axis=0, tiled=True)
    selected = jnp.take(every_row, track_index, axis=0)
    head_f = jnp.dot(masked, selected, preferred_element_type=jnp.float32)
    head_gradient = head_f.astype(jnp.bfloat16)
    padded_input = with_halo(head_gradient, (("seq", 0),), DILATION_SPAN).astype(jnp.float32)
    skip_act, pullback = jax.vjp(gelu_tanh, tok_f)
    convback = jnp.zeros(tok_f.shape, jnp.float32)
    tap_terms = []
    for shift_amount in range(3):
        shifted_rows = padded_input[
            DILATION_SPAN * (2 - shift_amount) : DILATION_SPAN * (2 - shift_amount) + token_rows
        ]
        convback = convback + dec_weight[shift_amount][None, :] * shifted_rows
        tap_terms.append(jnp.sum(skip_act * shifted_rows, axis=0))
    skip_grad = pullback(convback)[0].astype(jnp.bfloat16)
    summed = lax.psum(jnp.stack(tap_terms, axis=0), "seq")
    dec_weight_grad = summed / jnp.float32(math.sqrt(token_rows * lax.axis_size("seq")))
    return (skip_grad, dec_weight_grad)


def shards(
    enc_input,
    enc_weight,
    norm_gain,
    q_weight,
    kv_weight,
    out_weight,
    dec_weight,
    track_weight,
    track_grad,
    track_index,
    track_mask,
):
    token_rows = enc_input.shape[0] // 2
    patches = enc_input.reshape(token_rows, 2 * enc_input.shape[1])
    tok_sum = jnp.dot(
        patches,
        lax.all_gather(enc_weight, "seq", axis=0, tiled=True),
        preferred_element_type=jnp.float32,
    )
    tokens = tok_sum.astype(jnp.bfloat16)
    tok_f = tokens.astype(jnp.float32)
    trunk_out = attention(tokens, tok_f, norm_gain, q_weight, kv_weight, out_weight)
    skip_grad, dec_weight_grad = decoder_back(
        tok_f, dec_weight, track_weight, track_grad, track_index, track_mask
    )
    return (trunk_out, skip_grad, dec_weight_grad)


def solution(mesh):
    return jax.shard_map(
        shards,
        mesh=mesh,
        in_specs=(
            P(("groups", "seq"), None),
            P("seq", None),
            P(),
            P(),
            P(),
            P(),
            P(),
            P("seq", None),
            P("groups", "seq"),
            P("groups"),
            P("groups"),
        ),
        out_specs=(P(("groups", "seq"), None), P(("groups", "seq"), None), P("groups", None)),
        check_vma=False,
    )
```

profile of v0, /device:TPU:0, one launch (start us, length us, event | category | flops | bytes accessed | tf_op | source)
XLA Modules:
  0.0 272.7 jit_solution(8789962556055584525)
XLA Ops:
  7.9 1.1 copy.22
  9.6 7.4 %all-to-all-start = ((bf16[16,128,12]{1,2,0:T(8,128)(2,1)}), bf16[16,128,12]{1,2,0:T(8,128)(2,1)S(1)}, u32[]{:S(2)}, u32[]{:S(2)}) async-start(bf16[16,128,12]{1,2,0:T(8,128)(2,1)} %copy.20), calls=%async_computation | async-start | bytes 131072 | tf_op jit(solution)/shard_map/all_to_all | solution.py:84
  17.1 30.1 %all-gather = bf16[16,12,1536]{2,1,0:T(8,128)(2,1)} all-gather(bf16[1,12,1536]{2,1,0:T(8,128)(2,1)} %bitcast.28), channel_id=1, replica_groups=mesh['groups'=2,'seq'=16] {'seq'}, dimensions={0}, use_global_device_ids=true | all-gather | bytes 626688 | tf_op jit(solution)/shard_map/all_gather | solution.py:86
  47.2 2.0 reshape.51
  51.3 3.6 %gather_fusion = bf16[192,1536]{1,0:T(8,128)(2,1)} fusion(bf16[192,1536]{1,0:T(8,128)(2,1)} %reshape.51, s32[1024]{0:T(1024)S(1)} %pad_clamp_fusion), kind=kCustom, calls=%fused_computation | custom fusion | bytes 1180416 | tf_op jit(solution)/shard_map/jit(_take)/gather | solution.py:87
  55.5 1.5 convolution_convert_fusion.1
  57.7 2.8 %collective-permute-start = (bf16[8,1536]{1,0:T(8,128)(2,1)}, bf16[8,1536]{1,0:T(8,128)(2,1)}, u32[]{:S(2)}, u32[]{:S(2)}) collective-permute-start(bf16[8,1536]{1,0:T(8,128)(2,1)} %get-tuple-element.101), channel_id=1, source_target_pairs={{0,1},{1,2},{2,3},{3,4},{4,5},{5,6},{6,7},{7,8},{8,9},{9,10},{10,1... | collective-permute-start | bytes 73736 | tf_op jit(solution)/shard_map/ppermute | solution.py:21
  60.5 1.3 collective-permute-start.1
  61.7 1.5 slice_reduce_fusion.2
  63.2 2.1 reshape.38
  65.4 1.8 maximum_convert_fusion
  67.2 26.1 %all-gather.4.cloned.1.call-done = bf16[2816,1536]{1,0:T(8,128)(2,1)} async-done(((bf16[176,1536]{1,0:T(8,128)(2,1)}), bf16[2816,1536]{1,0:T(8,128)(2,1)}) %all-gather.4.cloned.1.call-update) | async-done | bytes 8650768 | tf_op jit(solution)/shard_map/all_gather | solution.py:123
  93.3 7.5 %multiply_reduce_fusion.3 = (f32[1536]{0:T(1024)S(1)}, f32[1536]{0:T(1024)S(1)}, f32[1536]{0:T(1024)S(1)}, f32[128]{0:T(128)S(1)}, bf16[128,1536]{1,0:T(8,128)(2,1)}, /*index=5*/f32[128,1536]{1,0:T(8,128)S(1)}) fusion(f32[144,1536]{1,0:T(8,128)} %maximum_convert_fusion, f32[1536]{0:T(1024)S(1)} %get-tuple-element.82, f32[1536]{0:T(1024)} %get-tuple-element.83, ...), kind=kOutput, calls=%fused_computation.34 | convolution fusion | flops 1114172800 | bytes 12947968 | tf_op jit(solution)/shard_map/dot_general | solution.py:121
  101.6 1.1 convolution_convert_fusion.3
  102.8 2.5 convolution_convert_fusion.2
  105.3 1.1 reshape.40
  106.4 59.2 %psum.7 = f32[3,1536]{1,0:T(4,128)S(1)} all-reduce(f32[3,1536]{1,0:T(4,128)S(1)} %pad_maximum_fusion), channel_id=1, replica_groups=mesh['groups'=2,'seq'=16] {'seq'}, use_global_device_ids=true, to_apply=%region_8.9 | all-reduce | flops 4608 | bytes 36864 | tf_op jit(solution)/shard_map/psum | solution.py:101
  166.2 2.6 copy.21
  168.7 89.4 %while.15 = (s32[]{:T(128)}, f32[1024]{0:T(1024)S(1)}, f32[1024]{0:T(1024)S(1)}, f32[1024,192]{0,1:T(8,128)}, bf16[16,128,320]{2,1,0:T(8,128)(2,1)}, /*index=5*/bf16[1024,128]{1,0:T(8,128)(2,1)S(1)}, s32[]{:T(128)}, s32[]{:T(128)}) while((s32[]{:T(128)}, f32[1024]{0:T(1024)S(1)}, f32[1024]{0:T(1024)S(1)}, f32[1024,192]{0,1:T(8,128)}, ...), condition=%wide.region_4.5_spmd.clone, body=%wide.region_1.4_spmd.clone.sunk | while | flops 85267456 | bytes 3735653 | solution.py:72
  169.7 1.0 fusion.40
  170.7 1.1 fusion.41
  171.9 2.2 convolution_add_fusion.3
  175.0 1.0 fusion.40
  176.1 1.1 fusion.41
  177.2 2.5 convolution_add_fusion.3
  180.6 1.0 fusion.40
  181.7 1.1 fusion.41
  182.8 2.5 convolution_add_fusion.3
  186.2 1.0 fusion.40
  187.3 1.1 fusion.41
  188.4 2.5 convolution_add_fusion.3
  191.8 1.0 fusion.40
  192.9 1.1 fusion.41
  194.0 2.5 convolution_add_fusion.3
  197.4 1.0 fusion.40
  198.5 1.1 fusion.41
  199.6 2.5 convolution_add_fusion.3
  203.0 1.0 fusion.40
  204.1 1.1 fusion.41
  205.2 2.5 convolution_add_fusion.3
  208.6 1.0 fusion.40
  209.7 1.1 fusion.41
  210.8 2.5 convolution_add_fusion.3
  214.2 1.0 fusion.40
  215.3 1.1 fusion.41
  216.4 2.5 convolution_add_fusion.3
  219.8 1.0 fusion.40
  220.9 1.1 fusion.41
  222.0 2.5 convolution_add_fusion.3
  226.5 1.1 fusion.41
  227.6 2.5 convolution_add_fusion.3
  232.1 1.1 fusion.41
  233.2 2.5 convolution_add_fusion.3
  237.7 1.1 fusion.41
  238.8 2.5 convolution_add_fusion.3
  243.3 1.1 fusion.41
  244.4 2.5 convolution_add_fusion.3
  248.9 1.1 fusion.41
  250.0 2.5 convolution_add_fusion.3
  254.5 1.1 fusion.41
  255.6 2.5 convolution_add_fusion.3
  258.1 1.2 divide_convert_fusion
  260.3 1.5 convert_element_type.46
  261.8 4.1 %fusion.8 = bf16[128,1536]{1,0:T(8,128)(2,1)} fusion(f32[128,1536]{1,0:T(8,128)} %copy-done.1, bf16[128,1536]{1,0:T(8,128)(2,1)S(1)} %convert_element_type.46, bf16[1536,1536]{1,0:T(8,128)(2,1)} %param.18), kind=kOutput, calls=%fused_computation.19 | convolution fusion | flops 604372992 | bytes 6291456 | tf_op jit(solution)/shard_map/dot_general | solution.py:77
  (104 shorter events, 28.3 us)
Async XLA Ops:
  7.2 95.6 %copy-start = (bf16[1536,1024]{1,0:T(8,128)(2,1)S(1)}, bf16[1536,1024]{1,0:T(8,128)(2,1)}, u32[]{:S(2)}) copy-start(bf16[1536,1024]{1,0:T(8,128)(2,1)} %param.16) | copy-start | bytes 9437188
  7.2 86.1 %all-gather.4.cloned.1.call-start = ((), (), s32[]{:S(2)}) async-start(), calls=%async_computation.1 | async-start | bytes 9191424 | tf_op jit(solution)/shard_map/all_gather | solution.py:123
  9.6 45.3 %all-to-all-start = ((bf16[16,128,12]{1,2,0:T(8,128)(2,1)}), bf16[16,128,12]{1,2,0:T(8,128)(2,1)S(1)}, u32[]{:S(2)}, u32[]{:S(2)}) async-start(bf16[16,128,12]{1,2,0:T(8,128)(2,1)} %copy.20), calls=%async_computation | async-start | bytes 131072 | tf_op jit(solution)/shard_map/all_to_all | solution.py:84
  17.0 149.2 %all-gather.6.cloned.1.call-start = ((), (), s32[]{:S(2)}) async-start(), calls=%async_computation.2 | async-start | bytes 1392640 | tf_op jit(solution)/shard_map/all_gather | solution.py:66
  57.7 7.7 %collective-permute-start = (bf16[8,1536]{1,0:T(8,128)(2,1)}, bf16[8,1536]{1,0:T(8,128)(2,1)}, u32[]{:S(2)}, u32[]{:S(2)}) collective-permute-start(bf16[8,1536]{1,0:T(8,128)(2,1)} %get-tuple-element.101), channel_id=1, source_target_pairs={{0,1},{1,2},{2,3},{3,4},{4,5},{5,6},{6,7},{7,8},{8,9},{9,10},{10,1... | collective-permute-start | bytes 73736 | tf_op jit(solution)/shard_map/ppermute | solution.py:21
  60.5 4.9 %collective-permute-start.1 = (bf16[8,1536]{1,0:T(8,128)(2,1)}, bf16[8,1536]{1,0:T(8,128)(2,1)}, u32[]{:S(2)}, u32[]{:S(2)}) collective-permute-start(bf16[8,1536]{1,0:T(8,128)(2,1)} %get-tuple-element.102), channel_id=1, source_target_pairs={{1,0},{2,1},{3,2},{4,3},{5,4},{6,5},{7,6},{8,7},{9,8},{10,9},{11,1... | collective-permute-start | bytes 73736 | tf_op jit(solution)/shard_map/ppermute | solution.py:23
  93.3 8.3 %copy-start.2 = (bf16[1536,320]{0,1:T(8,128)(2,1)S(1)}, bf16[1536,320]{0,1:T(8,128)(2,1)}, u32[]{:S(2)}) copy-start(bf16[1536,320]{0,1:T(8,128)(2,1)} %param.17) | copy-start | bytes 2949124
  93.3 8.3 %copy-start.3 = (f32[1536]{0:T(1024)S(1)}, f32[1536]{0:T(1024)}, u32[]{:S(2)}) copy-start(f32[1536]{0:T(1024)} %param.15) | copy-start | bytes 18436
  100.7 0.9 copy-start.1
Sparse Core Ops, SparseCore 0:
  10.3 82.9 all-gather.3
  102.9 36.2 all-gather.5
where the time goes:
time: 275 us; the launch traced here: 273 us
  blocking collectives  89.3 us (32%)
  matrix products  72.9 us (27%)
  local copies, waits for them, and re-layouts  33.7 us (12%)
  waiting for transfers between devices  26.8 us (10%)
  other arithmetic  24.2 us (9%)
  between operations  14.2 us (5%)
  starting transfers between devices  11.6 us (4%)
    psum x1, blocking collectives, decoder_back(): summed = lax.psum(jnp.stack(tap_terms, axis=0), 'seq')  59.2 us
    dot_general x16, matrix products, block_update(): jnp.dot(expw.astype(jnp.bfloat16), key_block[:, QK:], preferred_element_t...  39.6 us
    all_gather x1, blocking collectives, decoder_back(): every_row = lax.all_gather(track_weight, 'seq', axis=0, tiled=True)  30.1 us
    all_gather x1, waiting for transfers between devices, shards(): lax.all_gather(enc_weight, 'seq', axis=0, tiled=True)  26.1 us
    reduce_sum x16, other arithmetic, block_update(): running_sum = running_sum * shrink + jnp.sum(expw, axis=1)  18.2 us
    dot_general x16, matrix products, block_update(): lax.dot_general(query_rows, key_block[:, :QK], (((1,), (1,)), ((), ())),...  16.7 us
    squeeze x16, local copies, waits for them, and re-layouts, attention(): lax.scan(step_fn, carry, piece.reshape(count // 128, 128, piece.shape[1]))  14.4 us
    dot_general x1, matrix products, shards(): jnp.dot(patches, lax.all_gather(enc_weight, 'seq', axis=0, tiled=True), p...  7.46 us
  transfers between devices with their start and end apart: 5, of which 1 were waited for; matrix products, arithmetic and copies ran while one was open for 8% of the time, Pallas kernels for 0%

commit v1 on v0

--- a/solution.py
+++ b/solution.py
@@ -8,6 +8,19 @@
 QK = 128
 VDIM = 192
 DILATION_SPAN = 8
+
+
+def save_shelves(view):
+    local_now, reached = (jax.lax.axis_size("seq"), jax.lax.axis_index("seq"))
+    out_arr, moved = (view, 1)
+    while moved < local_now:
+        block_next = tuple(((dev_j, dev_j ^ moved) for dev_j in range(local_now)))
+        opened = jax.lax.ppermute(out_arr, "seq", block_next)
+        arr_next = jnp.concatenate([out_arr, opened], 0)
+        response = jnp.concatenate([opened, out_arr], axis=0)
+        out_arr = jnp.where(reached & moved == 0, arr_next, response)
+        moved = 2 * moved
+    return out_arr
 
 
 def with_halo(cells, sides, width):
@@ -118,11 +131,7 @@
 ):
     token_rows = enc_input.shape[0] // 2
     patches = enc_input.reshape(token_rows, 2 * enc_input.shape[1])
-    tok_sum = jnp.dot(
-        patches,
-        lax.all_gather(enc_weight, "seq", axis=0, tiled=True),
-        preferred_element_type=jnp.float32,
-    )
+    tok_sum = jnp.dot(patches, save_shelves(enc_weight), preferred_element_type=jnp.float32)
     tokens = tok_sum.astype(jnp.bfloat16)
     tok_f = tokens.astype(jnp.float32)
     trunk_out = attention(tokens, tok_f, norm_gain, q_weight, kv_weight, out_weight)

time: 275 us -> 505 us (1.84)
  blocking collectives: 89.3 us -> 258 us
  waiting for transfers between devices: 26.8 us -> 73.5 us
  other arithmetic: 24.2 us -> 33.6 us
    all_gather x1, blocking collectives: 30.1 us -> 194 us  [decoder_back(): every_row = lax.all_gather(track_weight, 'seq', axis=0, tiled=True)]
    ppermute x0 -> x4, waiting for transfers between devices: none -> 73.5 us  [save_shelves(): opened = jax.lax.ppermute(out_arr, 'seq', block_next)]
    all_gather x1 -> x0, waiting for transfers between devices: 26.1 us -> none  [shards(): lax.all_gather(enc_weight, 'seq', axis=0, tiled=True)]
    select_n x0 -> x3, other arithmetic: none -> 12.5 us  [save_shelves(): out_arr = jnp.where(reached & moved == 0, arr_next, response)]
    ppermute x0 -> x4, starting transfers between devices: none -> 7.7 us  [save_shelves(): opened = jax.lax.ppermute(out_arr, 'seq', block_next)]
    psum x1, blocking collectives: 59.2 us -> 64.6 us  [decoder_back(): summed = lax.psum(jnp.stack(tap_terms, axis=0), 'seq')]
  transfers between devices with their start and end apart: 5 -> 8, of which waited for: 1 -> 3; matrix products, arithmetic and copies ran while one was open for 8% -> 3% of each run, Pallas kernels for 0% -> 0%
where the time goes in v1:
time: 505 us; the launch traced here: 503 us
  blocking collectives  258 us (51%)
  matrix products  74.3 us (15%)
  waiting for transfers between devices  73.5 us (15%)
  other arithmetic  33.6 us (7%)
  local copies, waits for them, and re-layouts  32.8 us (6%)
  starting transfers between devices  15.8 us (3%)
  between operations  14.2 us (3%)
    all_gather x1, blocking collectives, decoder_back(): every_row = lax.all_gather(track_weight, 'seq', axis=0, tiled=True)  194 us
    ppermute x4, waiting for transfers between devices, save_shelves(): opened = jax.lax.ppermute(out_arr, 'seq', block_next)  73.5 us
    psum x1, blocking collectives, decoder_back(): summed = lax.psum(jnp.stack(tap_terms, axis=0), 'seq')  64.6 us
    dot_general x16, matrix products, block_update(): jnp.dot(expw.astype(jnp.bfloat16), key_block[:, QK:], preferred_element_t...  39.7 us
    reduce_sum x16, other arithmetic, block_update(): running_sum = running_sum * shrink + jnp.sum(expw, axis=1)  18.2 us
    dot_general x16, matrix products, block_update(): lax.dot_general(query_rows, key_block[:, :QK], (((1,), (1,)), ((), ())),...  16.7 us
    squeeze x16, local copies, waits for them, and re-layouts, attention(): lax.scan(step_fn, carry, piece.reshape(count // 128, 128, piece.shape[1]))  14.4 us
    select_n x3, other arithmetic, save_shelves(): out_arr = jnp.where(reached & moved == 0, arr_next, response)  12.5 us
  transfers between devices with their start and end apart: 8, of which 3 were waited for; matrix products, arithmetic and copies ran while one was open for 3% of the time, Pallas kernels for 0%

profile of v1, /device:TPU:0, one launch (start us, length us, event | category | flops | bytes accessed | tf_op | source)
XLA Modules:
  0.0 502.7 jit_solution(72258049865572238)
XLA Ops:
  7.7 1.9 collective-permute-done
  9.6 2.8 maximum_select_fusion.10
  12.4 2.9 collective-permute-start.1
  15.3 24.5 %collective-permute-done.1 = bf16[352,1536]{1,0:T(8,128)(2,1)} collective-permute-done((bf16[352,1536]{1,0:T(8,128)(2,1)}, bf16[352,1536]{1,0:T(8,128)(2,1)}, u32[]{:S(2)}, u32[]{:S(2)}) %collective-permute-start.1) | collective-permute-done | bytes 1081376 | tf_op jit(solution)/shard_map/ppermute | solution.py:18
  39.7 4.2 maximum_select_fusion.9
  43.9 1.8 collective-permute-start.2
  45.7 47.1 %collective-permute-done.2 = bf16[704,1536]{1,0:T(8,128)(2,1)} collective-permute-done((bf16[704,1536]{1,0:T(8,128)(2,1)}, bf16[704,1536]{1,0:T(8,128)(2,1)}, u32[]{:S(2)}, u32[]{:S(2)}) %collective-permute-start.2) | collective-permute-done | bytes 2162720 | tf_op jit(solution)/shard_map/ppermute | solution.py:18
  92.8 5.5 %maximum_select_fusion.2 = bf16[1408,1536]{1,0:T(8,128)(2,1)} fusion(bf16[704,1536]{1,0:T(8,128)(2,1)} %collective-permute-done.2, bf16[704,1536]{1,0:T(8,128)(2,1)} %maximum_select_fusion.9, pred[]{:T(512)S(6)} %eq.13), kind=kLoop, calls=%fused_computation.23 | loop fusion | flops 19464192 | bytes 8650753 | tf_op jit(solution)/shard_map/jit(_where)/select_n | solution.py:21
  98.3 2.5 collective-permute-start.3
  101.5 3.9 all-to-all-start
  105.5 193.8 %all-gather = bf16[16,12,1536]{2,1,0:T(8,128)(2,1)} all-gather(bf16[1,12,1536]{2,1,0:T(8,128)(2,1)S(1)} %bitcast.29), channel_id=1, replica_groups=mesh['groups'=2,'seq'=16] {'seq'}, dimensions={0}, use_global_device_ids=true | all-gather | bytes 626688 | tf_op jit(solution)/shard_map/all_gather | solution.py:99
  299.3 2.0 reshape.51
  301.4 3.6 gather_fusion
  305.6 1.5 convolution_convert_fusion
  307.7 2.8 collective-permute-start.4
  310.6 1.3 collective-permute-start.5
  311.9 1.5 slice_reduce_fusion.2
  313.4 2.2 reshape.38
  316.4 8.8 %multiply_reduce_fusion.3 = (f32[1536]{0:T(1024)S(1)}, f32[1536]{0:T(1024)S(1)}, f32[1536]{0:T(1024)S(1)}, f32[128]{0:T(128)S(1)}, bf16[128,1536]{1,0:T(8,128)(2,1)}, /*index=5*/f32[128,1536]{1,0:T(8,128)S(1)}) fusion(f32[144,1536]{1,0:T(8,128)S(1)} %maximum_convert_fusion, f32[1536]{0:T(1024)S(1)} %get-tuple-element.82, f32[1536]{0:T(1024)} %get-tuple-element.83, ...), kind=kOutput, calls=%fused_computation.46 | convolution fusion | flops 1153101184 | bytes 12947969 | tf_op jit(solution)/shard_map/dot_general | solution.py:134
  326.1 1.1 convolution_convert_fusion.2
  327.3 2.5 convolution_convert_fusion.1
  329.8 1.1 reshape.40
  330.9 64.6 %psum.7 = f32[3,1536]{1,0:T(4,128)S(1)} all-reduce(f32[3,1536]{1,0:T(4,128)S(1)} %pad_maximum_fusion), channel_id=1, replica_groups=mesh['groups'=2,'seq'=16] {'seq'}, use_global_device_ids=true, to_apply=%region_8.9 | all-reduce | flops 4608 | bytes 36864 | tf_op jit(solution)/shard_map/psum | solution.py:114
  396.1 2.6 copy.21
  398.6 89.4 %while.15 = (s32[]{:T(128)}, f32[1024]{0:T(1024)S(1)}, f32[1024]{0:T(1024)S(1)}, f32[1024,192]{0,1:T(8,128)}, bf16[16,128,320]{2,1,0:T(8,128)(2,1)}, /*index=5*/bf16[1024,128]{1,0:T(8,128)(2,1)S(1)}, s32[]{:T(128)}, s32[]{:T(128)}) while((s32[]{:T(128)}, f32[1024]{0:T(1024)S(1)}, f32[1024]{0:T(1024)S(1)}, f32[1024,192]{0,1:T(8,128)}, ...), condition=%wide.region_4.5_spmd.clone, body=%wide.region_1.4_spmd.clone.sunk | while | flops 85267456 | bytes 3735653 | solution.py:85
  399.5 1.0 fusion.49
  400.6 1.1 fusion.50
  401.7 2.2 convolution_add_fusion.3
  404.9 1.0 fusion.49
  405.9 1.1 fusion.50
  407.1 2.5 convolution_add_fusion.3
  411.5 1.1 fusion.50
  412.7 2.5 convolution_add_fusion.3
  416.1 1.0 fusion.49
  417.1 1.1 fusion.50
  418.3 2.5 convolution_add_fusion.3
  422.8 1.1 fusion.50
  423.9 2.5 convolution_add_fusion.3
  427.3 1.0 fusion.49
  428.4 1.1 fusion.50
  429.5 2.5 convolution_add_fusion.3
  434.0 1.1 fusion.50
  435.1 2.5 convolution_add_fusion.3
  439.6 1.1 fusion.50
  440.7 2.5 convolution_add_fusion.3
  445.2 1.1 fusion.50
  446.3 2.5 convolution_add_fusion.3
  450.8 1.1 fusion.50
  451.9 2.5 convolution_add_fusion.3
  456.4 1.1 fusion.50
  457.5 2.5 convolution_add_fusion.3
  462.0 1.1 fusion.50
  463.1 2.5 convolution_add_fusion.3
  467.6 1.1 fusion.50
  468.7 2.5 convolution_add_fusion.3
  473.2 1.1 fusion.50
  474.3 2.5 convolution_add_fusion.3
  478.8 1.1 fusion.50
  479.9 2.5 convolution_add_fusion.3
  484.4 1.1 fusion.50
  485.5 2.5 convolution_add_fusion.3
  488.0 1.2 divide_convert_fusion
  490.2 1.5 convert_element_type.51
  491.8 4.1 fusion.17
  (120 shorter events, 33.2 us)
Async XLA Ops:
  7.2 320.1 %copy-start = (bf16[1536,1024]{1,0:T(8,128)(2,1)S(1)}, bf16[1536,1024]{1,0:T(8,128)(2,1)}, u32[]{:S(2)}) copy-start(bf16[1536,1024]{1,0:T(8,128)(2,1)} %param.16) | copy-start | bytes 9437188
  7.2 2.4 collective-permute-start
  12.4 27.4 %collective-permute-start.1 = (bf16[352,1536]{1,0:T(8,128)(2,1)}, bf16[352,1536]{1,0:T(8,128)(2,1)}, u32[]{:S(2)}, u32[]{:S(2)}) collective-permute-start(bf16[352,1536]{1,0:T(8,128)(2,1)} %maximum_select_fusion.10), channel_id=1, source_target_pairs={{0,2},{1,3},{2,0},{3,1},{4,6},{5,7},{6,4},{7,5},{8,10},{9,11},{10,... | collective-permute-start | bytes 3244040 | tf_op jit(solution)/shard_map/ppermute | solution.py:18
  43.9 48.9 %collective-permute-start.2 = (bf16[704,1536]{1,0:T(8,128)(2,1)}, bf16[704,1536]{1,0:T(8,128)(2,1)}, u32[]{:S(2)}, u32[]{:S(2)}) collective-permute-start(bf16[704,1536]{1,0:T(8,128)(2,1)} %maximum_select_fusion.9), channel_id=1, source_target_pairs={{0,4},{1,5},{2,6},{3,7},{4,0},{5,1},{6,2},{7,3},{8,12},{9,13},{10,... | collective-permute-start | bytes 6488072 | tf_op jit(solution)/shard_map/ppermute | solution.py:18
  45.7 55.1 %copy-start.3 = (bf16[2048,12]{0,1:T(8,128)(2,1)S(1)}, bf16[2048,12]{0,1:T(8,128)(2,1)}, u32[]{:S(2)}) copy-start(bf16[2048,12]{0,1:T(8,128)(2,1)} %param.21) | copy-start | bytes 147460
  45.7 59.7 %copy-start.4 = (bf16[12,1536]{1,0:T(8,128)(2,1)S(1)}, bf16[12,1536]{1,0:T(8,128)(2,1)}, u32[]{:S(2)}) copy-start(bf16[12,1536]{1,0:T(8,128)(2,1)} %param.20) | copy-start | bytes 110596
  45.7 255.6 %copy-start.7 = (s32[192]{0:T(256)S(1)}, s32[192]{0:T(256)}, u32[]{:S(2)}) copy-start(s32[192]{0:T(256)} %param.23) | copy-start | bytes 2308
  45.7 255.6 %copy-start.6 = (s32[192]{0:T(256)S(1)}, s32[192]{0:T(256)}, u32[]{:S(2)}) copy-start(s32[192]{0:T(256)} %param.22) | copy-start | bytes 2308
  98.3 218.1 %collective-permute-start.3 = (bf16[1408,1536]{1,0:T(8,128)(2,1)}, bf16[1408,1536]{1,0:T(8,128)(2,1)}, u32[]{:S(2)}, u32[]{:S(2)}) collective-permute-start(bf16[1408,1536]{1,0:T(8,128)(2,1)} %maximum_select_fusion.2), channel_id=1, source_target_pairs={{0,8},{1,9},{2,10},{3,11},{4,12},{5,13},{6,14},{7,15},{8,0},{9,1},... | collective-permute-start | bytes 12976136 | tf_op jit(solution)/shard_map/ppermute | solution.py:18
  101.5 203.5 %all-to-all-start = ((bf16[16,128,12]{1,2,0:T(8,128)(2,1)}), bf16[16,128,12]{1,2,0:T(8,128)(2,1)S(1)}, u32[]{:S(2)}, u32[]{:S(2)}) async-start(bf16[16,128,12]{1,2,0:T(8,128)(2,1)} %copy.20), calls=%async_computation | async-start | bytes 131072 | tf_op jit(solution)/shard_map/all_to_all | solution.py:97
  105.4 290.6 %all-gather.3.cloned.1.call-start = ((), (), s32[]{:S(2)}) async-start(), calls=%async_computation.1 | async-start | bytes 1392640 | tf_op jit(solution)/shard_map/all_gather | solution.py:79
  307.7 7.8 %collective-permute-start.4 = (bf16[8,1536]{1,0:T(8,128)(2,1)}, bf16[8,1536]{1,0:T(8,128)(2,1)}, u32[]{:S(2)}, u32[]{:S(2)}) collective-permute-start(bf16[8,1536]{1,0:T(8,128)(2,1)} %get-tuple-element.101), channel_id=1, source_target_pairs={{0,1},{1,2},{2,3},{3,4},{4,5},{5,6},{6,7},{7,8},{8,9},{9,10},{10,1... | collective-permute-start | bytes 73736 | tf_op jit(solution)/shard_map/ppermute | solution.py:34
  310.6 5.0 collective-permute-start.5
  316.4 9.7 %copy-start.2 = (bf16[1536,320]{0,1:T(8,128)(2,1)S(1)}, bf16[1536,320]{0,1:T(8,128)(2,1)}, u32[]{:S(2)}) copy-start(bf16[1536,320]{0,1:T(8,128)(2,1)} %param.17) | copy-start | bytes 2949124
  316.4 9.7 %copy-start.5 = (f32[1536]{0:T(1024)S(1)}, f32[1536]{0:T(1024)}, u32[]{:S(2)}) copy-start(f32[1536]{0:T(1024)} %param.15) | copy-start | bytes 18436
  325.2 0.9 copy-start.1
Sparse Core Ops, SparseCore 0:
  327.3 41.9 all-gather.2
